TPU v7x, 32 devices: a whole 2x2x4 slice. The times are simulated.
32 devices in a mesh: dp: 8 (over y, x, core), mp: 4 (over z).
Axes of the slice: x: 2, y: 2, z: 4, core: 2. Of those that a mesh axis runs over, the one named last changes fastest.
Arguments:
- hidden: bfloat16 [192, 256, 4096], P(('dp', 'mp')), may hold values from -6 to 6
- lengths: int32 [192], P(('dp', 'mp')), may hold values from 32 to 256, as said below
- list_ids: int32 [192], P('dp'), may hold values from 0 to 65535, as said below
- gain: bfloat16 [4096], replicated, may hold values from 0.099609375 to 1.8984375
- head: bfloat16 [4096, 1024], P('dp', 'mp'), may hold values from -0.09375 to 0.09375
- list_slot: int32 [65536], replicated, may hold values from 0 to 65535, as said below
- centroids: bfloat16 [65536, 1024], P('dp'), may hold values from -0.59765625 to 0.59765625
- rotation: bfloat16 [1024, 1024], P('mp'), may hold values from -0.1875 to 0.1875
Outputs:
- codes: bfloat16 [192, 1024], P('dp', 'mp')
- scales: bfloat16 [192, 16], P('dp', 'mp')
Inputs may be any that keep to these rules, and one draw needn't show every extreme that they name: `list_ids`: in each aligned block of 24 passages, at most 6 have lists in one range of 8192 lists (list id // 8192); one range holds exactly 6 of them in every block. Each list's row in the centroid table; list_slot[l] // 8192 equals l // 8192, and each row of a range once. `lengths`: some passage has exactly 256 valid tokens.
All inputs are finite; a program needn't handle non-finite values. Where the computation divides by a largest or mean magnitude, that divisor is 1e-20 or more.
Results may differ from a plain program's by a relative error of at most 0.013.
Values may be sent and summed in bfloat16 or wider, within the bound.
No kernel may reach another device: no remote copies, remote signals or barrier semaphores. Data moves between devices by JAX's collectives and lax.ppermute only.
A program may use at most 64 MiB of HBM per device.

v0:
```python
import jax
import jax.numpy as jnp
from jax import lax
from jax.sharding import PartitionSpec as P

BLOCK = 64


def quantize(rotated):
    lead = rotated.shape[:-1]
    width = rotated.shape[-1]
    blocks = rotated.reshape(lead + (width // BLOCK, BLOCK))
    scale = jnp.max(jnp.abs(blocks), axis=-1) + 1e-06
    codes = (blocks / scale[..., None]).reshape(lead + (width,)).astype(jnp.bfloat16)
    return (codes, scale.astype(jnp.bfloat16))


def pick_own(placing, buckets):
    picked = jnp.einsum("poc,oce->pe", placing, buckets, preferred_element_type=jnp.float32)
    return picked.astype(buckets.dtype)


def per_device(hidden, lengths, list_ids, gain, head, list_slot, centroids, rotation):
    passes, slots, width = hidden.shape
    states = hidden.astype(jnp.float32)
    mean_square = jnp.mean(states * states, axis=-1)
    valid = jnp.arange(slots, dtype=jnp.int32)[None, :] < lengths[:, None]
    weights = (
        jnp.where(valid, lax.rsqrt(mean_square + 1e-05), 0.0) / lengths.astype(jnp.float32)[:, None]
    )
    pooled_mine = (jnp.einsum("pl,pld->pd", weights, states) * gain.astype(jnp.float32)).astype(
        jnp.bfloat16
    )
    pooled = lax.all_gather(pooled_mine, "mp", axis=0, tiled=True)
    group = pooled.shape[0]
    col_width = head.shape[1]
    projected = jnp.dot(
        pooled, lax.all_gather(head, "dp", axis=0, tiled=True), preferred_element_type=jnp.float32
    ).astype(jnp.bfloat16)
    owners = lax.axis_size("dp")
    lists_own = centroids.shape[0]
    capacity = max(2, 2 * group // owners)
    col_start = lax.axis_index("mp") * col_width
    cent_cols = lax.dynamic_slice_in_dim(centroids, col_start, col_width, 1)
    owner = list_ids // lists_own
    local_row = list_slot[list_ids] % lists_own
    matches = (owner[:, None] == jnp.arange(owners, dtype=jnp.int32)[None, :]).astype(jnp.int32)
    earlier = jnp.cumsum(matches, axis=0) - matches
    rank = jnp.sum(earlier * matches, axis=1)
    placed = (matches[:, :, None] > 0) & (
        rank[:, None, None] == jnp.arange(capacity, dtype=jnp.int32)[None, None, :]
    )
    placing = placed.astype(jnp.bfloat16)
    bucket_ids = jnp.sum(jnp.where(placed, local_row[:, None, None], 0), axis=0)
    cents_back = lax.all_to_all(
        cent_cols[lax.all_to_all(bucket_ids, "dp", split_axis=0, concat_axis=0, tiled=True)],
        "dp",
        split_axis=0,
        concat_axis=0,
        tiled=True,
    )
    cents = pick_own(placing, cents_back)
    resid = (projected.astype(jnp.float32) - cents.astype(jnp.float32)).astype(jnp.bfloat16)
    partial_value = jnp.dot(resid, rotation, preferred_element_type=jnp.float32)
    rotated = lax.psum_scatter(partial_value, "mp", scatter_dimension=1, tiled=True)
    codes, scales = quantize(rotated)
    return (codes, scales)


def solution(mesh):
    in_specs = (
        P(("dp", "mp"), None, None),
        P(("dp", "mp")),
        P("dp"),
        P(),
        P("dp", "mp"),
        P(),
        P("dp", None),
        P("mp", None),
    )
    out_specs = (P("dp", "mp"), P("dp", "mp"))
    return jax.shard_map(
        per_device, mesh=mesh, in_specs=in_specs, out_specs=out_specs, check_vma=False
    )
```

profile of v0, /device:TPU:0, one launch (start us, length us, event | category | flops | bytes accessed | tf_op | source)
XLA Modules:
  0.0 92.6 jit_solution(1821076101298347327)
XLA Ops:
  7.2 0.0 copy-start
  7.2 0.0 copy-start.2
  7.2 0.0 copy-start.1
  7.2 0.7 and_select_fusion.2
  7.9 0.1 fusion.16
  8.0 0.2 select_reduce_fusion
  8.2 0.1 copy.16
  8.3 1.7 %gather_fusion = s32[24]{0:T(128)S(1)} fusion(s32[65536]{0:T(1024)} %param.13, s32[1024]{0:T(1024)S(1)} %pad_clamp_fusion.1), kind=kCustom, calls=%fused_computation | custom fusion | bytes 288 | tf_op jit(solution)/shard_map/gather | solution.py:46
  10.0 0.8 fusion.10
  10.8 5.2 %all-to-all-start = ((s32[8,1,6]{2,1,0:T(1,128)}), s32[8,1,6]{2,1,0:T(1,128)S(1)}, u32[]{:S(2)}, u32[]{:S(2)}) async-start(s32[8,1,6]{2,1,0:T(1,128)} %bitcast.4), calls=%async_computation | async-start | bytes 8192 | tf_op jit(solution)/shard_map/all_to_all | solution.py:56
  16.0 0.0 all-gather.3.cloned.1.call-start
  16.1 0.7 all-gather.3.cloned.1.call-update
  16.7 7.1 %multiply_reduce_fusion = f32[6,256]{1,0:T(8,128)S(1)} fusion(bf16[6,256,4096]{2,1,0:T(8,128)(2,1)} %param.8), kind=kLoop, calls=%fused_computation.2 | loop fusion | flops 18872832 | bytes 12589056 | tf_op jit(solution)/shard_map/reduce_sum | solution.py:26
  23.8 0.0 copy-done.2
  23.8 0.0 copy-done.1
  23.9 0.1 divide_bitcast_fusion
  23.9 6.5 %fusion.17 = f32[6,1,4096]{2,1,0:T(1,128)S(1)} fusion(bf16[6,256,4096]{2,1,0:T(8,128)(2,1)} %param.8, bf16[6,256,1]{1,0,2:T(8,128)(2,1)S(1)} %divide_bitcast_fusion), kind=kOutput, calls=%fused_computation.27 | convolution fusion | flops 12582912 | bytes 12684288 | tf_op jit(solution)/shard_map/pl,pld->pd/dot_general | solution.py:31
  30.4 0.1 fusion.7
  30.5 4.4 %constant_dynamic-slice_fusion = bf16[8192,256]{1,0:T(8,128)(2,1)} fusion(bf16[8192,1024]{1,0:T(8,128)(2,1)} %param.14, s32[]{:T(128)S(6)} %select_n.42), kind=kLoop, calls=%fused_computation.42 | loop fusion | bytes 8388612 | tf_op jit(solution)/shard_map/dynamic_slice | solution.py:44
  34.9 14.2 %all-gather = bf16[4,6,4096]{2,1,0:T(8,128)(2,1)S(1)} all-gather(bf16[1,6,4096]{2,1,0:T(8,128)(2,1)S(1)} %fusion.7), channel_id=1, replica_groups=mesh['dp'=8,'mp'=4] {'mp'}, dimensions={0}, use_global_device_ids=true | all-gather | bytes 245760 | tf_op jit(solution)/shard_map/all_gather | solution.py:34
  49.1 0.1 reshape.121
  49.2 0.0 all-to-all-done
  49.2 0.1 copy.18
  49.3 0.1 copy.19
  49.4 0.1 reshape.112
  49.5 3.4 %gather_fusion.1 = bf16[48,256]{1,0:T(8,128)(2,1)S(1)} fusion(bf16[8192,256]{1,0:T(8,128)(2,1)} %constant_dynamic-slice_fusion, s32[1024]{0:T(1024)S(1)} %pad_clamp_fusion), kind=kCustom, calls=%fused_computation.1 | custom fusion | bytes 49344 | tf_op jit(solution)/shard_map/gather | solution.py:56
  52.9 0.6 reshape.111
  53.5 4.0 %all-to-all-start.1 = ((bf16[8,6,256]{2,1,0:T(8,128)(2,1)}), bf16[8,6,256]{2,1,0:T(8,128)(2,1)S(1)}, u32[]{:S(2)}, u32[]{:S(2)}) async-start(bf16[8,6,256]{2,1,0:T(8,128)(2,1)} %reshape.111), calls=%async_computation.1 | async-start | bytes 65536 | tf_op jit(solution)/shard_map/all_to_all | solution.py:55
  57.5 0.0 reduce-scatter.2.cloned.1.call-start
  57.5 0.0 all-gather.3.cloned.1.call-done
  57.5 2.0 %fusion.4 = f32[24,256]{1,0:T(8,128)S(1)} fusion(bf16[24,4096]{1,0:T(8,128)(2,1)S(1)} %reshape.121, bf16[4096,256]{1,0:T(8,128)(2,1)} %all-gather.3.cloned.1.call-done), kind=kOutput, calls=%fused_computation.9 | convolution fusion | flops 50343936 | bytes 2318336 | tf_op jit(solution)/shard_map/dot_general | solution.py:37
  59.5 2.8 %all-to-all-done.1 = bf16[8,6,256]{2,1,0:T(8,128)(2,1)S(1)} async-done(((bf16[8,6,256]{2,1,0:T(8,128)(2,1)}), bf16[8,6,256]{2,1,0:T(8,128)(2,1)S(1)}, u32[]{:S(2)}, u32[]{:S(2)}) %all-to-all-start.1) | async-done | bytes 24608 | tf_op jit(solution)/shard_map/all_to_all | solution.py:55
  62.3 0.0 copy-done
  62.3 1.0 %fusion.5 = f32[24,1024]{1,0:T(8,128)} fusion(bf16[256,1024]{1,0:T(8,128)(2,1)S(1)} %copy-done, f32[24,256]{1,0:T(8,128)S(1)} %fusion.4, bf16[8,6,256]{2,1,0:T(8,128)(2,1)S(1)} %all-to-all-done.1, pred[24,6]{0,1:T(8,128)(4,1)S(1)} %iota_compare_fusion.2, pred[24,8]{0,1:T(8,128)(4,1)S(1)} %copy.16), kind=kOutput, calls=%fused_computation.10 | convolution fusion | flops 13198464 | bytes 672080 | tf_op jit(solution)/shard_map/dot_general | solution.py:64
  63.3 0.0 reduce-scatter.2.cloned.1.call-update
  63.3 19.3 %reduce-scatter.2.cloned.1.call-done = f32[24,256]{1,0:T(8,128)} async-done(((f32[24,1024]{1,0:T(8,128)}), f32[24,256]{1,0:T(8,128)}) %reduce-scatter.2.cloned.1.call-update) | async-done | bytes 24592 | tf_op jit(solution)/shard_map/reduce_scatter | solution.py:65
  82.6 0.7 abs.6
  83.3 0.1 abs.7
  83.4 0.1 reduce_max.9
  83.5 0.1 div.45
  83.6 0.1 div.46
  83.7 0.7 copy.20
  84.4 1.3 %divide_convert_fusion = bf16[24,256]{1,0:T(8,128)(2,1)} fusion(f32[24,256]{1,0:T(8,128)} %reduce-scatter.2.cloned.1.call-done, f32[24,256]{1,0:T(8,128)S(1)} %div.46), kind=kLoop, calls=%fused_computation.17 | loop fusion | flops 12288 | bytes 61440 | tf_op jit(solution)/shard_map/convert_element_type | solution.py:14
  (9 shorter events, 0.1 us)
Async XLA Ops:
  7.2 55.2 %copy-start = (bf16[256,1024]{1,0:T(8,128)(2,1)S(1)}, bf16[256,1024]{1,0:T(8,128)(2,1)}, u32[]{:S(2)}) copy-start(bf16[256,1024]{1,0:T(8,128)(2,1)} %param.15) | copy-start | bytes 1572868
  7.2 16.6 %copy-start.2 = (s32[6]{0:T(128)S(1)}, s32[6]{0:T(128)}, u32[]{:S(2)}) copy-start(s32[6]{0:T(128)} %param.9) | copy-start | bytes 76
  7.2 16.6 %copy-start.1 = (bf16[4096]{0:T(1024)(128)(2,1)S(1)}, bf16[4096]{0:T(1024)(128)(2,1)}, u32[]{:S(2)}) copy-start(bf16[4096]{0:T(1024)(128)(2,1)} %param.11) | copy-start | bytes 24580
  10.8 38.4 %all-to-all-start = ((s32[8,1,6]{2,1,0:T(1,128)}), s32[8,1,6]{2,1,0:T(1,128)S(1)}, u32[]{:S(2)}, u32[]{:S(2)}) async-start(s32[8,1,6]{2,1,0:T(1,128)} %bitcast.4), calls=%async_computation | async-start | bytes 8192 | tf_op jit(solution)/shard_map/all_to_all | solution.py:56
  16.0 41.5 %all-gather.3.cloned.1.call-start = ((), (), s32[]{:S(2)}) async-start(), calls=%async_computation.3 | async-start | bytes 2359296 | tf_op jit(solution)/shard_map/all_gather | solution.py:38
  53.5 8.8 %all-to-all-start.1 = ((bf16[8,6,256]{2,1,0:T(8,128)(2,1)}), bf16[8,6,256]{2,1,0:T(8,128)(2,1)S(1)}, u32[]{:S(2)}, u32[]{:S(2)}) async-start(bf16[8,6,256]{2,1,0:T(8,128)(2,1)} %reshape.111), calls=%async_computation.1 | async-start | bytes 65536 | tf_op jit(solution)/shard_map/all_to_all | solution.py:55
  57.5 25.1 %reduce-scatter.2.cloned.1.call-start = ((), (), s32[]{:S(2)}) async-start(), calls=%async_computation.4 | async-start | bytes 122880 | tf_op jit(solution)/shard_map/reduce_scatter | solution.py:65
Sparse Core Ops, SparseCore 0:
  18.7 29.4 all-gather.2
  63.4 19.0 reduce-scatter.1
where the time goes:
time: 93.2 us; the launch traced here: 92.6 us
  waiting for transfers between devices  22.8 us (24%)
  blocking collectives  14.2 us (15%)
  between operations  14.2 us (15%)
  local copies, waits for them, and re-layouts  11.4 us (12%)
  other arithmetic  11.3 us (12%)
  matrix products  9.46 us (10%)
  starting transfers between devices  9.28 us (10%)
    reduce_scatter x1, waiting for transfers between devices, per_device(): lax.psum_scatter(partial_value, 'mp', scatter_dimension=1, tiled=True)  19.3 us
    all_gather x1, blocking collectives, per_device(): pooled = lax.all_gather(pooled_mine, 'mp', axis=0, tiled=True)  14.2 us
    reduce_sum x1, other arithmetic, per_device(): mean_square = jnp.mean(states * states, axis=-1)  7.07 us
    dot_general x1, matrix products, per_device(): jnp.einsum('pl,pld->pd', weights, states) * gain.astype(jnp.float32)  6.5 us
    all_to_all x1, starting transfers between devices, per_device(): lax.all_to_all(bucket_ids, 'dp', split_axis=0, concat_axis=0, tiled=True)  5.2 us
    dynamic_slice x1, local copies, waits for them, and re-layouts, per_device(): cent_cols = lax.dynamic_slice_in_dim(centroids, col_start, col_width, 1)  4.4 us
    all_to_all x1, starting transfers between devices, per_device(): lax.all_to_all(cent_cols[lax.all_to_all(bucket_ids, 'dp', split_axis=0, c...  4.01 us
    gather x2, local copies, waits for them, and re-layouts, per_device(): cent_cols[lax.all_to_all(bucket_ids, 'dp', split_axis=0, concat_axis=0, t...  3.97 us
  transfers between devices with their start and end apart: 4, of which 2 were waited for; matrix products, arithmetic and copies ran while one was open for 26% of the time, Pallas kernels for 0%

commit v1 on v0

--- a/solution.py
+++ b/solution.py
@@ -31,7 +31,12 @@
     pooled_mine = (jnp.einsum("pl,pld->pd", weights, states) * gain.astype(jnp.float32)).astype(
         jnp.bfloat16
     )
-    pooled = lax.all_gather(pooled_mine, "mp", axis=0, tiled=True)
+    ring = [pooled_mine]
+    for hop in range(3):
+        ring.append(lax.ppermute(ring[-1], "mp", [(dev, (dev + 1) % 4) for dev in range(4)]))
+    pooled = jnp.roll(
+        jnp.concatenate(ring[::-1], axis=0), (lax.axis_index("mp") + 1) * ring[0].shape[0], axis=0
+    )
     group = pooled.shape[0]
     col_width = head.shape[1]
     projected = jnp.dot(

time: 93.2 us -> 85.6 us (0.918)
  blocking collectives: 14.2 us -> 0 us
  starting transfers between devices: 9.28 us -> 14.1 us
    all_gather x1 -> x0, blocking collectives: 14.2 us -> none  [per_device(): pooled = lax.all_gather(pooled_mine, 'mp', axis=0, tiled=True)]
    ppermute x0 -> x3, starting transfers between devices: none -> 4.75 us  [per_device(): lax.ppermute(ring[-1], 'mp', [(dev, (dev + 1) % 4) for dev in range(4)])]
    dot_general x1, matrix products: 0.98 us -> 2.92 us  [per_device(): partial_value = jnp.dot(resid, rotation, preferred_element_type=jnp.float32)]
    dot_general x1, matrix products: 1.98 us -> 0.2 us  [pick_own(): jnp.einsum('poc,oce->pe', placing, buckets, preferred_element_type=jnp.fl...]
    ppermute x0 -> x3, waiting for transfers between devices: none -> 1.47 us  [per_device(): lax.ppermute(ring[-1], 'mp', [(dev, (dev + 1) % 4) for dev in range(4)])]
    reduce_scatter x1, waiting for transfers between devices: 19.3 us -> 18.2 us  [per_device(): lax.psum_scatter(partial_value, 'mp', scatter_dimension=1, tiled=True)]
  transfers between devices with their start and end apart: 4 -> 7, of which waited for: 2 -> 4; matrix products, arithmetic and copies ran while one was open for 26% -> 28% of each run, Pallas kernels for 0% -> 0%
where the time goes in v1:
time: 85.6 us; the launch traced here: 85 us
  waiting for transfers between devices  23.5 us (27%)
  between operations  14.2 us (17%)
  starting transfers between devices  14.1 us (16%)
  local copies, waits for them, and re-layouts  12.3 us (14%)
  other arithmetic  11.3 us (13%)
  matrix products  9.62 us (11%)
    reduce_scatter x1, waiting for transfers between devices, per_device(): lax.psum_scatter(partial_value, 'mp', scatter_dimension=1, tiled=True)  18.2 us
    reduce_sum x1, other arithmetic, per_device(): mean_square = jnp.mean(states * states, axis=-1)  7.07 us
    dot_general x1, matrix products, per_device(): jnp.einsum('pl,pld->pd', weights, states) * gain.astype(jnp.float32)  6.5 us
    all_to_all x1, starting transfers between devices, per_device(): lax.all_to_all(bucket_ids, 'dp', split_axis=0, concat_axis=0, tiled=True)  5.2 us
    ppermute x3, starting transfers between devices, per_device(): lax.ppermute(ring[-1], 'mp', [(dev, (dev + 1) % 4) for dev in range(4)])  4.75 us
    dynamic_slice x1, local copies, waits for them, and re-layouts, per_device(): cent_cols = lax.dynamic_slice_in_dim(centroids, col_start, col_width, 1)  4.4 us
    all_to_all x1, starting transfers between devices, per_device(): lax.all_to_all(cent_cols[lax.all_to_all(bucket_ids, 'dp', split_axis=0, c...  4.12 us
    gather x2, local copies, waits for them, and re-layouts, per_device(): cent_cols[lax.all_to_all(bucket_ids, 'dp', split_axis=0, concat_axis=0, t...  4.1 us
  transfers between devices with their start and end apart: 7, of which 4 were waited for; matrix products, arithmetic and copies ran while one was open for 28% of the time, Pallas kernels for 0%

profile of v1, /device:TPU:0, one launch (start us, length us, event | category | flops | bytes accessed | tf_op | source)
XLA Modules:
  0.0 85.0 jit_solution(15736643241290237987)
XLA Ops:
  7.2 0.0 copy-start
  7.2 0.0 copy-start.2
  7.2 0.0 copy-start.1
  7.2 0.7 and_select_fusion.2
  7.9 0.1 fusion.14
  8.0 0.2 select_reduce_fusion
  8.2 0.1 copy.16
  8.3 1.7 %gather_fusion = s32[24]{0:T(128)S(1)} fusion(s32[65536]{0:T(1024)} %param.13, s32[1024]{0:T(1024)S(1)} %pad_clamp_fusion.1), kind=kCustom, calls=%fused_computation | custom fusion | bytes 288 | tf_op jit(solution)/shard_map/gather | solution.py:51
  10.0 0.8 fusion.10
  10.8 5.2 %all-to-all-start = ((s32[8,1,6]{2,1,0:T(1,128)}), s32[8,1,6]{2,1,0:T(1,128)S(1)}, u32[]{:S(2)}, u32[]{:S(2)}) async-start(s32[8,1,6]{2,1,0:T(1,128)} %bitcast.3), calls=%async_computation | async-start | bytes 8192 | tf_op jit(solution)/shard_map/all_to_all | solution.py:61
  16.0 0.0 all-gather.2.cloned.1.call-start
  16.1 0.7 all-gather.2.cloned.1.call-update
  16.7 7.1 %multiply_reduce_fusion = f32[6,256]{1,0:T(8,128)S(1)} fusion(bf16[6,256,4096]{2,1,0:T(8,128)(2,1)} %param.8), kind=kLoop, calls=%fused_computation.2 | loop fusion | flops 18872832 | bytes 12589056 | tf_op jit(solution)/shard_map/reduce_sum | solution.py:26
  23.8 0.0 copy-done.2
  23.8 0.0 copy-done.1
  23.8 0.1 divide_bitcast_fusion
  23.9 6.5 %fusion.15 = f32[6,1,4096]{2,1,0:T(1,128)S(1)} fusion(bf16[6,256,4096]{2,1,0:T(8,128)(2,1)} %param.8, bf16[6,256,1]{1,0,2:T(8,128)(2,1)S(1)} %divide_bitcast_fusion), kind=kOutput, calls=%fused_computation.27 | convolution fusion | flops 12582912 | bytes 12684288 | tf_op jit(solution)/shard_map/pl,pld->pd/dot_general | solution.py:31
  30.4 0.1 fusion.8
  30.5 1.6 %collective-permute-start = (bf16[6,4096]{1,0:T(8,128)(2,1)S(1)}, bf16[6,4096]{1,0:T(8,128)(2,1)S(1)}, u32[]{:S(2)}, u32[]{:S(2)}) collective-permute-start(bf16[6,4096]{1,0:T(8,128)(2,1)S(1)} %fusion.8), channel_id=1, source_target_pairs={{0,1},{1,2},{2,3},{3,0},{4,5},{5,6},{6,7},{7,4},{8,9},{9,10},{10,1... | collective-permute-start | bytes 147464 | tf_op jit(solution)/shard_map/ppermute | solution.py:36
  32.1 4.4 %constant_dynamic-slice_fusion = bf16[8192,256]{1,0:T(8,128)(2,1)} fusion(bf16[8192,1024]{1,0:T(8,128)(2,1)} %param.14, s32[]{:T(128)S(6)} %select_n.56), kind=kLoop, calls=%fused_computation.42 | loop fusion | bytes 8388612 | tf_op jit(solution)/shard_map/dynamic_slice | solution.py:49
  36.5 0.0 all-to-all-done
  36.5 0.1 copy.18
  36.6 0.1 copy.19
  36.7 0.1 reshape.112
  36.8 0.2 collective-permute-done
  36.9 1.5 %collective-permute-start.1 = (bf16[6,4096]{1,0:T(8,128)(2,1)S(1)}, bf16[6,4096]{1,0:T(8,128)(2,1)S(1)}, u32[]{:S(2)}, u32[]{:S(2)}) collective-permute-start(bf16[6,4096]{1,0:T(8,128)(2,1)S(1)} %collective-permute-done), channel_id=1, source_target_pairs={{0,1},{1,2},{2,3},{3,0},{4,5},{5,6},{6,7},{7,4},{8,9},{9,10},{10,1... | collective-permute-start | bytes 147464 | tf_op jit(solution)/shard_map/ppermute | solution.py:36
  38.4 3.5 %gather_fusion.1 = bf16[48,256]{1,0:T(8,128)(2,1)S(1)} fusion(bf16[8192,256]{1,0:T(8,128)(2,1)} %constant_dynamic-slice_fusion, s32[1024]{0:T(1024)S(1)} %pad_clamp_fusion), kind=kCustom, calls=%fused_computation.1 | custom fusion | bytes 49344 | tf_op jit(solution)/shard_map/gather | solution.py:61
  41.9 0.6 reshape.111
  42.5 4.1 %all-to-all-start.1 = ((bf16[8,6,256]{2,1,0:T(8,128)(2,1)}), bf16[8,6,256]{2,1,0:T(8,128)(2,1)S(1)}, u32[]{:S(2)}, u32[]{:S(2)}) async-start(bf16[8,6,256]{2,1,0:T(8,128)(2,1)} %reshape.111), calls=%async_computation.1 | async-start | bytes 65536 | tf_op jit(solution)/shard_map/all_to_all | solution.py:60
  46.6 0.0 reduce-scatter.2.cloned.1.call-start
  46.7 0.0 collective-permute-done.1
  46.7 1.7 %collective-permute-start.2 = (bf16[6,4096]{1,0:T(8,128)(2,1)S(1)}, bf16[6,4096]{1,0:T(8,128)(2,1)S(1)}, u32[]{:S(2)}, u32[]{:S(2)}) collective-permute-start(bf16[6,4096]{1,0:T(8,128)(2,1)S(1)} %collective-permute-done.1), channel_id=1, source_target_pairs={{0,1},{1,2},{2,3},{3,0},{4,5},{5,6},{6,7},{7,4},{8,9},{9,10},{10,1... | collective-permute-start | bytes 147464 | tf_op jit(solution)/shard_map/ppermute | solution.py:36
  48.4 3.1 %all-to-all-done.1 = bf16[8,6,256]{2,1,0:T(8,128)(2,1)S(1)} async-done(((bf16[8,6,256]{2,1,0:T(8,128)(2,1)}), bf16[8,6,256]{2,1,0:T(8,128)(2,1)S(1)}, u32[]{:S(2)}, u32[]{:S(2)}) %all-to-all-start.1) | async-done | bytes 24608 | tf_op jit(solution)/shard_map/all_to_all | solution.py:60
  51.5 0.2 fusion.1
  51.7 1.3 %collective-permute-done.2 = bf16[6,4096]{1,0:T(8,128)(2,1)S(1)} collective-permute-done((bf16[6,4096]{1,0:T(8,128)(2,1)S(1)}, bf16[6,4096]{1,0:T(8,128)(2,1)S(1)}, u32[]{:S(2)}, u32[]{:S(2)}) %collective-permute-start.2) | collective-permute-done | bytes 49184 | tf_op jit(solution)/shard_map/ppermute | solution.py:36
  53.0 0.8 concatenate.6
  53.8 0.0 all-gather.2.cloned.1.call-done
  53.9 0.0 copy-done
  53.9 2.9 %fusion.5 = f32[24,1024]{1,0:T(8,128)} fusion(bf16[256,1024]{1,0:T(8,128)(2,1)S(1)} %copy-done, f32[24,256]{1,0:T(8,128)S(1)} %fusion.1, bf16[4096,256]{1,0:T(8,128)(2,1)} %all-gather.2.cloned.1.call-done, bf16[48,4096]{1,0:T(8,128)(2,1)S(1)} %concatenate.6, s32[]{:T(128)S(6)} %select_n.54), kind=kOutput, calls=%fused_computation.10 | convolution fusion | flops 62939136 | bytes 2940932 | tf_op jit(solution)/shard_map/dot_general | solution.py:69
  56.8 0.0 reduce-scatter.2.cloned.1.call-update
  56.8 18.2 %reduce-scatter.2.cloned.1.call-done = f32[24,256]{1,0:T(8,128)} async-done(((f32[24,1024]{1,0:T(8,128)}), f32[24,256]{1,0:T(8,128)}) %reduce-scatter.2.cloned.1.call-update) | async-done | bytes 24592 | tf_op jit(solution)/shard_map/reduce_scatter | solution.py:70
  75.0 0.7 abs.6
  75.7 0.1 abs.7
  75.8 0.1 reduce_max.9
  76.0 0.1 div.45
  76.0 0.1 div.46
  76.1 0.7 copy.20
  76.8 1.3 %divide_convert_fusion = bf16[24,256]{1,0:T(8,128)(2,1)} fusion(f32[24,256]{1,0:T(8,128)} %reduce-scatter.2.cloned.1.call-done, f32[24,256]{1,0:T(8,128)S(1)} %div.46), kind=kLoop, calls=%fused_computation.17 | loop fusion | flops 12288 | bytes 61440 | tf_op jit(solution)/shard_map/convert_element_type | solution.py:14
  (9 shorter events, 0.1 us)
Async XLA Ops:
  7.2 46.7 %copy-start = (bf16[256,1024]{1,0:T(8,128)(2,1)S(1)}, bf16[256,1024]{1,0:T(8,128)(2,1)}, u32[]{:S(2)}) copy-start(bf16[256,1024]{1,0:T(8,128)(2,1)} %param.15) | copy-start | bytes 1572868
  7.2 16.6 %copy-start.2 = (s32[6]{0:T(128)S(1)}, s32[6]{0:T(128)}, u32[]{:S(2)}) copy-start(s32[6]{0:T(128)} %param.9) | copy-start | bytes 76
  7.2 16.6 %copy-start.1 = (bf16[4096]{0:T(1024)(128)(2,1)S(1)}, bf16[4096]{0:T(1024)(128)(2,1)}, u32[]{:S(2)}) copy-start(bf16[4096]{0:T(1024)(128)(2,1)} %param.11) | copy-start | bytes 24580
  10.8 25.7 %all-to-all-start = ((s32[8,1,6]{2,1,0:T(1,128)}), s32[8,1,6]{2,1,0:T(1,128)S(1)}, u32[]{:S(2)}, u32[]{:S(2)}) async-start(s32[8,1,6]{2,1,0:T(1,128)} %bitcast.3), calls=%async_computation | async-start | bytes 8192 | tf_op jit(solution)/shard_map/all_to_all | solution.py:61
  16.0 37.9 %all-gather.2.cloned.1.call-start = ((), (), s32[]{:S(2)}) async-start(), calls=%async_computation.3 | async-start | bytes 2359296 | tf_op jit(solution)/shard_map/all_gather | solution.py:43
  30.5 6.4 %collective-permute-start = (bf16[6,4096]{1,0:T(8,128)(2,1)S(1)}, bf16[6,4096]{1,0:T(8,128)(2,1)S(1)}, u32[]{:S(2)}, u32[]{:S(2)}) collective-permute-start(bf16[6,4096]{1,0:T(8,128)(2,1)S(1)} %fusion.8), channel_id=1, source_target_pairs={{0,1},{1,2},{2,3},{3,0},{4,5},{5,6},{6,7},{7,4},{8,9},{9,10},{10,1... | collective-permute-start | bytes 147464 | tf_op jit(solution)/shard_map/ppermute | solution.py:36
  36.9 9.8 %collective-permute-start.1 = (bf16[6,4096]{1,0:T(8,128)(2,1)S(1)}, bf16[6,4096]{1,0:T(8,128)(2,1)S(1)}, u32[]{:S(2)}, u32[]{:S(2)}) collective-permute-start(bf16[6,4096]{1,0:T(8,128)(2,1)S(1)} %collective-permute-done), channel_id=1, source_target_pairs={{0,1},{1,2},{2,3},{3,0},{4,5},{5,6},{6,7},{7,4},{8,9},{9,10},{10,1... | collective-permute-start | bytes 147464 | tf_op jit(solution)/shard_map/ppermute | solution.py:36
  42.5 9.0 %all-to-all-start.1 = ((bf16[8,6,256]{2,1,0:T(8,128)(2,1)}), bf16[8,6,256]{2,1,0:T(8,128)(2,1)S(1)}, u32[]{:S(2)}, u32[]{:S(2)}) async-start(bf16[8,6,256]{2,1,0:T(8,128)(2,1)} %reshape.111), calls=%async_computation.1 | async-start | bytes 65536 | tf_op jit(solution)/shard_map/all_to_all | solution.py:60
  46.6 28.4 %reduce-scatter.2.cloned.1.call-start = ((), (), s32[]{:S(2)}) async-start(), calls=%async_computation.4 | async-start | bytes 122880 | tf_op jit(solution)/shard_map/reduce_scatter | solution.py:70
  46.7 6.3 %collective-permute-start.2 = (bf16[6,4096]{1,0:T(8,128)(2,1)S(1)}, bf16[6,4096]{1,0:T(8,128)(2,1)S(1)}, u32[]{:S(2)}, u32[]{:S(2)}) collective-permute-start(bf16[6,4096]{1,0:T(8,128)(2,1)S(1)} %collective-permute-done.1), channel_id=1, source_target_pairs={{0,1},{1,2},{2,3},{3,0},{4,5},{5,6},{6,7},{7,4},{8,9},{9,10},{10,1... | collective-permute-start | bytes 147464 | tf_op jit(solution)/shard_map/ppermute | solution.py:36
Sparse Core Ops, SparseCore 0:
  18.7 29.4 all-gather.1
  56.9 18.0 reduce-scatter.1
